TPU v7x, 32 devices: a whole 2x2x4 slice. The times are simulated.
32 devices in a mesh: ctx: 8 (over z, x), fsdp: 4 (over y, core).
Axes of the slice: x: 2, y: 2, z: 4, core: 2. Of those that a mesh axis runs over, the one named last changes fastest.
Arguments:
- block_in: bfloat16 [4, 2048, 1024], P('fsdp', 'ctx'), may hold values from -6 to 6
- out_grad: bfloat16 [4, 2048, 1024], P('fsdp', 'ctx'), may hold values from -6 to 6
- w_query: bfloat16 [1024, 1024], P('fsdp'), may hold values from -0.1875 to 0.1875
- w_key: bfloat16 [1024, 1024], P('fsdp'), may hold values from -0.1875 to 0.1875
- w_value: bfloat16 [1024, 1024], P('fsdp'), may hold values from -0.1875 to 0.1875
- w_out: bfloat16 [1024, 1024], P('fsdp'), may hold values from -0.1875 to 0.1875
- norm_one: float32 [1024], replicated, may hold values from 0.25 to 1.75
- norm_two: float32 [1024], replicated, may hold values from 0.25 to 1.75
- w_gate: bfloat16 [1024, 2816], P('fsdp'), may hold values from -0.1875 to 0.1875
- w_up: bfloat16 [1024, 2816], P('fsdp'), may hold values from -0.1875 to 0.1875
- w_down: bfloat16 [2816, 1024], P('fsdp'), may hold values from -0.109375 to 0.109375
- norm_three: float32 [1024], replicated, may hold values from 0.25 to 1.75
- norm_four: float32 [1024], replicated, may hold values from 0.25 to 1.75
- prompt_len: int32 [4], replicated, may hold values from 512 to 1024, as said below
- cont_len: int32 [4, 2], replicated, may hold values from 257 to 512, as said below
- group_ids: int32 [4], replicated, may hold values from 0 to 3, each once
- cont_ids: int32 [4, 2], replicated, may hold values from 0 to 1, each once within a row
Outputs:
- block_out: bfloat16 [4, 2048, 1024], P('fsdp', 'ctx')
- in_grad: float32 [4, 2048, 1024], P('fsdp', 'ctx')
- grad_query: float32 [1024, 1024], P('fsdp')
- grad_key: float32 [1024, 1024], P('fsdp')
- grad_value: float32 [1024, 1024], P('fsdp')
- grad_out: float32 [1024, 1024], P('fsdp')
- grad_norm_one: float32 [1024], replicated
- grad_norm_two: float32 [1024], replicated
- grad_gate: float32 [1024, 2816], P('fsdp')
- grad_up: float32 [1024, 2816], P('fsdp')
- grad_down: float32 [2816, 1024], P('fsdp')
- grad_norm_three: float32 [1024], replicated
- grad_norm_four: float32 [1024], replicated
Inputs may be any that keep to these rules, and one draw needn't show every extreme that they name: `prompt_len`: in every draw some group's prompt has exactly 1024 tokens. `cont_len`: every group has a continuation of exactly 512 tokens. `group_ids`: A permutation of the groups. `cont_ids`: each row is a permutation of the continuation numbers.
All inputs are finite; a program needn't handle non-finite values.
Results may differ from a plain program's by a relative error of at most 0.023.
Values may be sent and summed in bfloat16 or wider, within the bound.
No kernel may reach another device: no remote copies, remote signals or barrier semaphores. Data moves between devices by JAX's collectives and lax.ppermute only.
A program may use at most 192 MiB of HBM per device.

v0:
```python
import math
import jax
import jax.numpy as jnp
from jax import lax
from jax.sharding import PartitionSpec as P

HEAD = 128
P_DEV = 128
CONT = 512
eps_norm = 1e-06
rope_base = 50000.0
masked_out = -1e30


def rms_norm(values, gain_vec):
    inverse = lax.rsqrt(jnp.mean(values * values, axis=-1, keepdims=True) + eps_norm)
    return (values * inverse * gain_vec, inverse)


def norm_back(values, inverse, gain_vec, upstream):
    weighted = upstream * gain_vec
    inner_mean = jnp.mean(values * weighted, axis=-1, keepdims=True)
    value_grad = inverse * weighted - values * inverse * inverse * inverse * inner_mean
    return (value_grad, jnp.sum(upstream * values * inverse, axis=0))


def rotate(values, position, turn_sign):
    seq_len = values.shape[0]
    half_size = HEAD // 2
    split_heads = values.reshape(seq_len, -1, HEAD)
    frequencies = rope_base ** (-2.0 * jnp.arange(half_size, dtype=jnp.float32) / HEAD)
    angles = position.astype(jnp.float32)[:, None] * frequencies[None, :]
    cosine = jnp.concatenate([jnp.cos(angles), jnp.cos(angles)], axis=-1)[:, None, :]
    sine_part = turn_sign * jnp.concatenate([jnp.sin(angles), jnp.sin(angles)], axis=-1)[:, None, :]
    turned = jnp.concatenate([-split_heads[..., half_size:], split_heads[..., :half_size]], axis=-1)
    return (split_heads * cosine + turned * sine_part).reshape(seq_len, -1)


def token_info(slot_index, prompt, prompt_size, slot_lens):
    in_cont = slot_index >= prompt
    rel_index = jnp.maximum(slot_index - prompt, 0)
    slot_of = jnp.where(in_cont, rel_index // CONT, -1)
    offset = rel_index % CONT
    slot_range = jnp.arange(slot_lens.shape[0], dtype=jnp.int32)
    slot_len = jnp.sum(
        jnp.where(slot_of[:, None] == slot_range[None, :], slot_lens[None, :], 0), axis=1
    )
    token_valid = jnp.where(in_cont, offset < slot_len, slot_index < prompt_size)
    position = jnp.where(in_cont, prompt_size + offset, slot_index)
    return (token_valid, slot_of, position)


def cross_dot(operand, partner):
    return lax.dot_general(
        operand, partner, (((0,), (0,)), ((), ())), preferred_element_type=jnp.float32
    )


def back_dot(operand, partner):
    return lax.dot_general(
        operand, partner, (((1,), (1,)), ((), ())), preferred_element_type=jnp.float32
    )


def keep_same(state):
    return state


def shards(
    block_in,
    out_grad,
    w_query,
    w_key,
    w_value,
    w_out,
    norm_one,
    norm_two,
    w_gate,
    w_up,
    w_down,
    norm_three,
    norm_four,
    prompt_len,
    cont_len,
    group_ids,
    cont_ids,
):
    local_rows = block_in.shape[1]
    model_width = block_in.shape[2]
    ff_width = w_gate.shape[1]
    ctx_size = lax.axis_size("ctx")
    group_rows = local_rows * ctx_size
    prompt = P_DEV * ctx_size
    head_count = model_width // HEAD
    score_scale = 1.0 / math.sqrt(HEAD)
    row_index = lax.axis_index("fsdp")
    groups = group_ids.shape[0]
    slot_count = cont_ids.shape[1]
    group_range = jnp.arange(groups, dtype=jnp.int32)
    own_group = jnp.sum(jnp.where(group_range == row_index, group_ids, 0))
    own_prompt = jnp.sum(jnp.where(group_range == own_group, prompt_len, 0))
    own_lens = jnp.sum(jnp.where((group_range == own_group)[:, None], cont_len, 0), axis=0)
    own_ids = jnp.sum(jnp.where((group_range == row_index)[:, None], cont_ids, 0), axis=0)
    slot_range = jnp.arange(slot_count, dtype=jnp.int32)
    slot_lens = jnp.sum(
        jnp.where(own_ids[:, None] == slot_range[None, :], own_lens[None, :], 0), axis=1
    )
    query_index = lax.axis_index("ctx") * local_rows + jnp.arange(local_rows, dtype=jnp.int32)
    key_index = jnp.arange(group_rows, dtype=jnp.int32)
    query_valid, query_slot, position = token_info(query_index, prompt, own_prompt, slot_lens)
    key_valid, key_slot, unused_pos = token_info(key_index, prompt, own_prompt, slot_lens)
    tokens = block_in[0].astype(jnp.float32)
    full_query, full_key, full_value, full_out = (
        lax.all_gather(w_query, "fsdp", axis=0, tiled=True),
        lax.all_gather(w_key, "fsdp", axis=0, tiled=True),
        lax.all_gather(w_value, "fsdp", axis=0, tiled=True),
        lax.all_gather(w_out, "fsdp", axis=0, tiled=True),
    )
    normed_full, inverse_one = rms_norm(tokens, norm_one)
    normed = normed_full.astype(jnp.bfloat16)
    queries = rotate(
        jnp.dot(normed, full_query, preferred_element_type=jnp.float32), position, 1.0
    ).astype(jnp.bfloat16)
    keys_local = rotate(
        jnp.dot(normed, full_key, preferred_element_type=jnp.float32), position, 1.0
    ).astype(jnp.bfloat16)
    values_local = jnp.dot(normed, full_value, preferred_element_type=jnp.float32).astype(
        jnp.bfloat16
    )
    all_keys, all_values = (
        lax.all_gather(keys_local, "ctx", axis=0, tiled=True),
        lax.all_gather(values_local, "ctx", axis=0, tiled=True),
    )
    key_block = math.gcd(group_rows, 512)
    block_count = group_rows // key_block
    blocks_in = (
        all_keys.reshape(block_count, key_block, head_count, HEAD),
        all_values.reshape(block_count, key_block, head_count, HEAD),
        key_valid.reshape(block_count, key_block),
        key_slot.reshape(block_count, key_block),
        key_index.reshape(block_count, key_block),
    )
    query_heads = queries.reshape(local_rows, head_count, HEAD)

    def mask_of(inputs):
        key_ids = inputs[4]
        return (
            query_valid[:, None]
            & inputs[2][None, :]
            & (key_ids[None, :] <= query_index[:, None])
            & ((key_ids[None, :] < prompt) | (inputs[3][None, :] == query_slot[:, None]))
        )

    def raw_scores(inputs):
        return (
            jnp.einsum("qhd,khd->hqk", query_heads, inputs[0], preferred_element_type=jnp.float32)
            * score_scale
        )

    def running(state_in, inputs):
        allowed = mask_of(inputs)

        def running_visit(state):
            row_top, exp_total = state
            scores = jnp.where(allowed[None], raw_scores(inputs), masked_out)
            new_top = jnp.maximum(row_top, jnp.max(scores, axis=-1, keepdims=True))
            exp_total = exp_total * jnp.exp(row_top - new_top) + jnp.sum(
                jnp.where(allowed[None], jnp.exp(scores - new_top), 0.0), axis=-1, keepdims=True
            )
            return (new_top, exp_total)

        return (lax.cond(jnp.any(allowed), running_visit, keep_same, state_in), None)

    start_top = jnp.full((head_count, local_rows, 1), -jnp.inf, jnp.float32)
    start_total = jnp.zeros((head_count, local_rows, 1), jnp.float32)
    (row_top, exp_total), unused = lax.scan(running, (start_top, start_total), blocks_in)
    has_keys = exp_total > 0.0
    log_total = jnp.where(has_keys, row_top + jnp.log(jnp.where(has_keys, exp_total, 1.0)), 0.0)

    def probs_of(inputs, allowed):
        return jnp.where(allowed[None], jnp.exp(raw_scores(inputs) - log_total), 0.0)

    def mix_step(accumulated, inputs):
        allowed = mask_of(inputs)

        def mix_visit(total):
            attn_probs = probs_of(inputs, allowed).astype(jnp.bfloat16)
            return total + jnp.einsum(
                "hqk,khd->qhd", attn_probs, inputs[1], preferred_element_type=jnp.float32
            )

        return (lax.cond(jnp.any(allowed), mix_visit, keep_same, accumulated), None)

    mixture, unused = lax.scan(
        mix_step, jnp.zeros((local_rows, head_count, HEAD), jnp.float32), blocks_in
    )
    valid_col = query_valid[:, None].astype(jnp.float32)
    attended = (mixture.reshape(local_rows, model_width) * valid_col).astype(jnp.bfloat16)
    branch = jnp.dot(attended, full_out, preferred_element_type=jnp.float32)
    branch_normed, inverse_two = rms_norm(branch, norm_two)
    middle = tokens + branch_normed
    full_gate, full_up, full_down = (
        lax.all_gather(w_gate, "fsdp", axis=0, tiled=True),
        lax.all_gather(w_up, "fsdp", axis=0, tiled=True),
        lax.all_gather(w_down, "fsdp", axis=0, tiled=True),
    )
    ff_normed, inverse_three = rms_norm(middle, norm_three)
    ff_input = ff_normed.astype(jnp.bfloat16)
    gate_pre = jnp.dot(ff_input, full_gate, preferred_element_type=jnp.float32)
    upward = jnp.dot(ff_input, full_up, preferred_element_type=jnp.float32)
    gate_sig = jax.nn.sigmoid(gate_pre)
    swish_out = gate_pre * gate_sig
    hidden = (swish_out * upward).astype(jnp.bfloat16)
    ff_out = jnp.dot(hidden, full_down, preferred_element_type=jnp.float32)
    out_normed, inverse_four = rms_norm(ff_out, norm_four)
    result = middle + out_normed
    upstream = out_grad[0].astype(jnp.float32)
    ff_out_full, grad_norm_four = norm_back(ff_out, inverse_four, norm_four, upstream)
    ff_out_grad = ff_out_full.astype(jnp.bfloat16)
    hidden_grad = back_dot(ff_out_grad, full_down)
    up_grad = (hidden_grad * swish_out).astype(jnp.bfloat16)
    gate_grad = (hidden_grad * upward * gate_sig * (1.0 + gate_pre * (1.0 - gate_sig))).astype(
        jnp.bfloat16
    )
    ff_in_grad = back_dot(gate_grad, full_gate) + back_dot(up_grad, full_up)
    middle_part, grad_norm_three = norm_back(middle, inverse_three, norm_three, ff_in_grad)
    middle_grad = upstream + middle_part
    branch_full, grad_norm_two = norm_back(branch, inverse_two, norm_two, middle_grad)
    branch_grad = branch_full.astype(jnp.bfloat16)
    attended_grad = back_dot(branch_grad, full_out).astype(jnp.bfloat16) * valid_col.astype(
        jnp.bfloat16
    )
    grad_heads = attended_grad.reshape(local_rows, head_count, HEAD)

    def delta_step(accumulated, inputs):
        allowed = mask_of(inputs)

        def delta_visit(total):
            attn_probs = probs_of(inputs, allowed)
            prob_grad = jnp.einsum(
                "qhd,khd->hqk", grad_heads, inputs[1], preferred_element_type=jnp.float32
            )
            return total + jnp.sum(attn_probs * prob_grad, axis=-1, keepdims=True)

        return (lax.cond(jnp.any(allowed), delta_visit, keep_same, accumulated), None)

    row_delta, unused = lax.scan(
        delta_step, jnp.zeros((head_count, local_rows, 1), jnp.float32), blocks_in
    )
    zero_part = jnp.zeros((key_block, head_count, HEAD), jnp.float32)

    def grad_step(accumulated, inputs):
        allowed = mask_of(inputs)

        def grad_visit(total):
            attn_probs = probs_of(inputs, allowed)
            prob_grad = jnp.einsum(
                "qhd,khd->hqk", grad_heads, inputs[1], preferred_element_type=jnp.float32
            )
            score_grad = (attn_probs * (prob_grad - row_delta)).astype(jnp.bfloat16)
            total = total + jnp.einsum(
                "hqk,khd->qhd", score_grad, inputs[0], preferred_element_type=jnp.float32
            )
            key_part = jnp.einsum(
                "hqk,qhd->khd", score_grad, query_heads, preferred_element_type=jnp.float32
            )
            value_part = jnp.einsum(
                "hqk,qhd->khd",
                attn_probs.astype(jnp.bfloat16),
                grad_heads,
                preferred_element_type=jnp.float32,
            )
            return (total, (key_part, value_part))

        def skip(total):
            return (total, (zero_part, zero_part))

        return lax.cond(jnp.any(allowed), grad_visit, skip, accumulated)

    query_acc, (key_parts, value_parts) = lax.scan(
        grad_step, jnp.zeros((local_rows, head_count, HEAD), jnp.float32), blocks_in
    )
    key_terms = key_parts.reshape(group_rows, model_width) * score_scale
    value_terms = value_parts.reshape(group_rows, model_width)
    key_sum, value_sum = (
        lax.psum_scatter(
            key_terms.astype(jnp.bfloat16), "ctx", scatter_dimension=0, tiled=True
        ).astype(jnp.float32),
        lax.psum_scatter(
            value_terms.astype(jnp.bfloat16), "ctx", scatter_dimension=0, tiled=True
        ).astype(jnp.float32),
    )
    query_grad = rotate(
        query_acc.reshape(local_rows, model_width) * score_scale, position, -1.0
    ).astype(jnp.bfloat16)
    key_grad = rotate(key_sum, position, -1.0).astype(jnp.bfloat16)
    value_grad = value_sum.astype(jnp.bfloat16)
    normed_grad = (
        back_dot(query_grad, full_query)
        + back_dot(key_grad, full_key)
        + back_dot(value_grad, full_value)
    )
    input_part, grad_norm_one = norm_back(tokens, inverse_one, norm_one, normed_grad)
    input_grad = middle_grad + input_part
    wide_pairs = (
        (normed, query_grad),
        (normed, key_grad),
        (normed, value_grad),
        (attended, branch_grad),
        (ff_input, gate_grad),
        (ff_input, up_grad),
    )

    def wide_term(selector):
        return jnp.concatenate(
            [cross_dot(selector(operand), partner) for operand, partner in wide_pairs], axis=1
        )

    wide_local = lax.psum_scatter(
        wide_term(lambda operand: operand).astype(jnp.bfloat16),
        "fsdp",
        scatter_dimension=0,
        tiled=True,
    )
    ff_local = lax.psum_scatter(
        cross_dot((lambda operand: operand)(hidden), ff_out_grad).astype(jnp.bfloat16),
        "fsdp",
        scatter_dimension=0,
        tiled=True,
    )
    wide_sum, ff_sum = (
        lax.psum(wide_local, "ctx").astype(jnp.float32),
        lax.psum(ff_local, "ctx").astype(jnp.float32),
    )
    gain_sums = lax.psum(
        jnp.stack([grad_norm_one, grad_norm_two, grad_norm_three, grad_norm_four]), ("ctx", "fsdp")
    )
    edge_two = 2 * model_width
    edge_three = 3 * model_width
    edge_four = 4 * model_width
    edge_five = 4 * model_width + ff_width
    return (
        result.astype(jnp.bfloat16)[None],
        input_grad[None],
        wide_sum[:, :model_width],
        wide_sum[:, model_width:edge_two],
        wide_sum[:, edge_two:edge_three],
        wide_sum[:, edge_three:edge_four],
        gain_sums[0],
        gain_sums[1],
        wide_sum[:, edge_four:edge_five],
        wide_sum[:, edge_five:],
        ff_sum,
        gain_sums[2],
        gain_sums[3],
    )


def solution(mesh):
    return jax.shard_map(
        shards,
        mesh=mesh,
        in_specs=(
            P("fsdp", "ctx", None),
            P("fsdp", "ctx", None),
            P("fsdp", None),
            P("fsdp", None),
            P("fsdp", None),
            P("fsdp", None),
            P(),
            P(),
            P("fsdp", None),
            P("fsdp", None),
            P("fsdp", None),
            P(),
            P(),
            P(),
            P(),
            P(),
            P(),
        ),
        out_specs=(
            P("fsdp", "ctx", None),
            P("fsdp", "ctx", None),
            P("fsdp", None),
            P("fsdp", None),
            P("fsdp", None),
            P("fsdp", None),
            P(),
            P(),
            P("fsdp", None),
            P("fsdp", None),
            P("fsdp", None),
            P(),
            P(),
        ),
        check_vma=False,
    )
```

profile of v0, /device:TPU:0, one launch (start us, length us, event | category | flops | bytes accessed | tf_op | source)
XLA Modules:
  0.0 1122.9 jit_solution(17604052558741267211)
XLA Ops:
  16.3 18.6 %all-gather.14.cloned.1.call-done = bf16[1024,1024]{1,0:T(8,128)(2,1)} async-done(((bf16[256,1024]{1,0:T(8,128)(2,1)}), bf16[1024,1024]{1,0:T(8,128)(2,1)}) %all-gather.14.cloned.1.call-update) | async-done | bytes 2097168 | tf_op jit(solution)/shard_map/all_gather | solution.py:114
  34.9 2.9 copy.85
  37.8 21.3 %all-gather.10.cloned.1.call-done = bf16[1024,1024]{1,0:T(8,128)(2,1)} async-done(((bf16[256,1024]{1,0:T(8,128)(2,1)}), bf16[1024,1024]{1,0:T(8,128)(2,1)}) %all-gather.10.cloned.1.call-update) | async-done | bytes 2097168 | tf_op jit(solution)/shard_map/all_gather | solution.py:115
  59.1 3.9 copy.83
  67.9 15.3 %all-gather.16.cloned.1.call-done = bf16[1024,1024]{1,0:T(8,128)(2,1)} async-done(((bf16[256,1024]{1,0:T(8,128)(2,1)}), bf16[1024,1024]{1,0:T(8,128)(2,1)}) %all-gather.16.cloned.1.call-update) | async-done | bytes 2097168 | tf_op jit(solution)/shard_map/all_gather | solution.py:116
  83.3 3.1 convolution_convert_fusion.6
  92.4 66.9 %all-gather.12.cloned.1.call-done = bf16[2048,1024]{1,0:T(8,128)(2,1)} async-done(((bf16[256,1024]{1,0:T(8,128)(2,1)}), bf16[2048,1024]{1,0:T(8,128)(2,1)}) %all-gather.12.cloned.1.call-update) | async-done | bytes 4194320 | tf_op jit(solution)/shard_map/all_gather | solution.py:131
  159.2 3.3 copy.128
  162.5 3.0 copy.88
  165.5 68.0 %all-gather.18.cloned.1.call-done = bf16[2048,1024]{1,0:T(8,128)(2,1)} async-done(((bf16[256,1024]{1,0:T(8,128)(2,1)}), bf16[2048,1024]{1,0:T(8,128)(2,1)}) %all-gather.18.cloned.1.call-update) | async-done | bytes 4194320 | tf_op jit(solution)/shard_map/all_gather | solution.py:132
  233.5 3.3 copy.129
  236.8 2.9 copy.90
  239.7 10.0 while.63
  241.3 3.1 conditional.16
  249.8 10.7 while.64
  251.5 3.6 conditional.17
  251.5 3.6 fusion.24
  267.4 33.4 %all-gather.22.cloned.1.call-done = bf16[1024,2816]{1,0:T(8,128)(2,1)} async-done(((bf16[256,2816]{1,0:T(8,128)(2,1)}), bf16[1024,2816]{1,0:T(8,128)(2,1)}) %all-gather.22.cloned.1.call-update) | async-done | bytes 5767184 | tf_op jit(solution)/shard_map/all_gather | solution.py:203
  300.8 6.0 fusion.145
  306.8 39.0 %all-gather.24.cloned.1.call-done = bf16[1024,2816]{1,0:T(8,128)(2,1)} async-done(((bf16[256,2816]{1,0:T(8,128)(2,1)}), bf16[1024,2816]{1,0:T(8,128)(2,1)}) %all-gather.24.cloned.1.call-update) | async-done | bytes 5767184 | tf_op jit(solution)/shard_map/all_gather | solution.py:204
  345.8 7.4 multiply_convert_fusion.3
  353.2 37.6 %all-gather.26.cloned.1.call-done = bf16[2816,1024]{1,0:T(8,128)(2,1)} async-done(((bf16[704,1024]{1,0:T(8,128)(2,1)}), bf16[2816,1024]{1,0:T(8,128)(2,1)}) %all-gather.26.cloned.1.call-update) | async-done | bytes 5767184 | tf_op jit(solution)/shard_map/all_gather | solution.py:205
  390.8 5.0 multiply_reduce_fusion.4
  398.1 6.0 multiply_convert_fusion.1
  410.5 11.4 %while.65 = (s32[]{:T(128)}, f32[8,256,1]{1,2,0:T(1,128)S(1)}, pred[256]{0:T(512)(128)(4,1)S(1)}, pred[4,512]{1,0:T(4,128)(4,1)S(1)}, s32[4,512]{1,0:T(4,128)S(1...) while((s32[]{:T(128)}, f32[8,256,1]{1,2,0:T(1,128)S(1)}, ...), condition=%wide.region_31.32_spmd.clone.clone, body=%wide.region_26.31_spmd.clone.clone.sunk | while | flops 543035136 | bytes 11857887 | solution.py:247
  412.2 4.5 conditional.18
  423.0 38.1 %while.66 = (s32[]{:T(128)}, f32[256,8,128]{2,0,1:T(8,128)}, f32[4,512,8,128]{3,1,2,0:T(8,128)}, bf16[4,512,8,128]{3,1,2,0:T(8,128)(2,1)}, pred[256]{0:T(512)(12...) while((s32[]{:T(128)}, f32[256,8,128]{2,0,1:T(8,128)}, ...), condition=%wide.region_36.37_spmd.clone.clone, body=%wide.region_32.36_spmd.clone.clone.sunk | while | flops 1353846528 | bytes 89568512 | solution.py:280
  424.6 9.4 conditional.19
  461.1 4.6 multiply_convert_fusion
  468.4 3.2 copy.136
  471.7 4.9 copy.108
  476.6 3.1 copy.135
  481.1 4.2 convolution_convert_fusion
  487.9 3.1 convolution_convert_fusion.2
  491.1 4.2 copy.112
  496.4 90.5 %reduce-scatter.5.cloned.1.call-done = bf16[256,1024]{1,0:T(8,128)(2,1)} async-done(((bf16[2048,1024]{1,0:T(8,128)(2,1)}), bf16[256,1024]{1,0:T(8,128)(2,1)}) %reduce-scatter.5.cloned.1.call-update) | async-done | bytes 524304 | tf_op jit(solution)/shard_map/reduce_scatter | solution.py:286
  601.1 3.9 copy.110
  605.0 73.9 %reduce-scatter.7.cloned.1.call-done = bf16[256,1024]{1,0:T(8,128)(2,1)} async-done(((bf16[2048,1024]{1,0:T(8,128)(2,1)}), bf16[256,1024]{1,0:T(8,128)(2,1)}) %reduce-scatter.7.cloned.1.call-update) | async-done | bytes 524304 | tf_op jit(solution)/shard_map/reduce_scatter | solution.py:289
  678.9 3.2 convolution_convert_fusion.3
  682.1 3.9 copy.111
  693.5 4.2 convert_dynamic-update-slice_fusion.1
  697.7 4.5 convert_dynamic-update-slice_fusion
  702.2 33.7 %reduce-scatter.11.cloned.1.call-done = bf16[704,1024]{1,0:T(8,128)(2,1)} async-done(((bf16[2816,1024]{1,0:T(8,128)(2,1)}), bf16[704,1024]{1,0:T(8,128)(2,1)}) %reduce-scatter.11.cloned.1.call-update) | async-done | bytes 1441808 | tf_op jit(solution)/shard_map/reduce_scatter | solution.py:325
  735.9 149.1 %reduce-scatter.9.cloned.1.call-done = bf16[256,9728]{1,0:T(8,128)(2,1)} async-done(((bf16[1024,9728]{1,0:T(8,128)(2,1)}), bf16[256,9728]{1,0:T(8,128)(2,1)}) %reduce-scatter.9.cloned.1.call-update) | async-done | bytes 4980752 | tf_op jit(solution)/shard_map/reduce_scatter | solution.py:319
  889.7 43.4 %psum.22 = f32[4,1024]{1,0:T(4,128)S(1)} all-reduce(f32[4,1024]{1,0:T(4,128)S(1)} %pad_maximum_fusion.2), channel_id=1, replica_groups=mesh['ctx'=8,'fsdp'=4] {'ctx','fsdp'}, use_global_device_ids=true, to_apply=%region_46.47 | all-reduce | flops 4096 | bytes 32768 | tf_op jit(solution)/shard_map/psum | solution.py:335
  935.0 172.4 %all-reduce.3.cloned.1.call-done = (bf16[256,9728]{1,0:T(8,128)(2,1)}, bf16[704,1024]{1,0:T(8,128)(2,1)}) async-done(((bf16[256,9728]{1,0:T(8,128)(2,1)}, bf16[704,1024]{1,0:T(8,128)(2,1)}), (bf16[256,9728]{1,0:T(8,128)(2,1)}, bf16[704,1024]{1,0:T(8,128)(2,1)})) %all-reduce.3.cloned.1.call-update) | async-done | bytes 6422544 | tf_op jit(solution)/shard_map/psum | solution.py:332
  1107.4 3.9 fusion.143
  1111.3 2.9 fusion.142
  (350 shorter events, 130.3 us)
Async XLA Ops:
  7.2 27.7 %all-gather.14.cloned.1.call-start = ((), (), s32[]{:S(2)}) async-start(), calls=%async_computation.6 | async-start | bytes 2621440 | tf_op jit(solution)/shard_map/all_gather | solution.py:114
  7.9 51.2 %all-gather.10.cloned.1.call-start = ((), (), s32[]{:S(2)}) async-start(), calls=%async_computation.4 | async-start | bytes 2621440 | tf_op jit(solution)/shard_map/all_gather | solution.py:115
  8.7 74.6 %all-gather.16.cloned.1.call-start = ((), (), s32[]{:S(2)}) async-start(), calls=%async_computation.7 | async-start | bytes 2621440 | tf_op jit(solution)/shard_map/all_gather | solution.py:116
  9.4 149.9 %all-gather.12.cloned.1.call-start = ((), (), s32[]{:S(2)}) async-start(), calls=%async_computation.5 | async-start | bytes 4718592 | tf_op jit(solution)/shard_map/all_gather | solution.py:131
  15.0 51.4 %copy-start.26 = (f32[256,128]{0,1:T(8,128)}, f32[256,128]{0,1:T(8,128)S(1)}, u32[]{:S(2)}) copy-start(f32[256,128]{0,1:T(8,128)S(1)} %get-tuple-element.1103) | copy-start | bytes 393220
  16.3 67.0 %copy-start.37 = (f32[256]{0:T(256)}, f32[256]{0:T(256)S(1)}, u32[]{:S(2)}) copy-start(f32[256]{0:T(256)S(1)} %add_rsqrt_fusion.3) | copy-start | bytes 3076
  34.9 28.1 %copy-start.3 = (bf16[1,256,1024]{2,1,0:T(8,128)(2,1)S(1)}, bf16[1,256,1024]{2,1,0:T(8,128)(2,1)}, u32[]{:S(2)}) copy-start(bf16[1,256,1024]{2,1,0:T(8,128)(2,1)} %param.33) | copy-start | bytes 1572868
  34.9 28.1 %copy-start.35 = (f32[1024]{0:T(1024)S(1)}, f32[1024]{0:T(1024)}, u32[]{:S(2)}) copy-start(f32[1024]{0:T(1024)} %param.39) | copy-start | bytes 12292
  67.9 22.3 %copy-start.43 = (s32[4,2]{0,1:T(2,128)S(1)}, s32[4,2]{0,1:T(2,128)}, u32[]{:S(2)}) copy-start(s32[4,2]{0,1:T(2,128)} %param.47) | copy-start | bytes 100
  67.9 22.3 %copy-start.44 = (s32[4,2]{0,1:T(2,128)S(1)}, s32[4,2]{0,1:T(2,128)}, u32[]{:S(2)}) copy-start(s32[4,2]{0,1:T(2,128)} %param.49) | copy-start | bytes 100
  67.9 165.6 %all-gather.18.cloned.1.call-start = ((), (), s32[]{:S(2)}) async-start(), calls=%async_computation.8 | async-start | bytes 4718592 | tf_op jit(solution)/shard_map/all_gather | solution.py:132
  86.4 176.7 %all-gather.20.cloned.1.call-start = ((), (), s32[]{:S(2)}) async-start(), calls=%async_computation.9 | async-start | bytes 2621440 | tf_op jit(solution)/shard_map/all_gather | solution.py:117
  87.0 213.8 %all-gather.22.cloned.1.call-start = ((), (), s32[]{:S(2)}) async-start(), calls=%async_computation.10 | async-start | bytes 7208960 | tf_op jit(solution)/shard_map/all_gather | solution.py:203
  87.8 258.0 %all-gather.24.cloned.1.call-start = ((), (), s32[]{:S(2)}) async-start(), calls=%async_computation.11 | async-start | bytes 7208960 | tf_op jit(solution)/shard_map/all_gather | solution.py:204
  88.5 302.3 %all-gather.26.cloned.1.call-start = ((), (), s32[]{:S(2)}) async-start(), calls=%async_computation.12 | async-start | bytes 7208960 | tf_op jit(solution)/shard_map/all_gather | solution.py:205
  89.3 497.7 %reduce-scatter.5.cloned.1.call-start = ((), (), s32[]{:S(2)}) async-start(), calls=%async_computation.13 | async-start | bytes 4718592 | tf_op jit(solution)/shard_map/reduce_scatter | solution.py:286
  260.5 5.5 copy-start.39
  261.8 4.6 copy-start.40
  390.8 7.3 slice-start.4
  390.8 5.0 copy-start.12
  390.8 5.0 copy-start.42
  390.8 7.3 slice-start.5
  396.8 7.4 slice-start
  396.8 9.1 slice-start.2
  398.1 6.1 copy-start.23
  398.1 6.1 slice-start.1
  398.1 7.8 slice-start.3
  424.7 4.7 copy-start.32
  435.6 3.8 copy-start.31
  442.8 3.8 copy-start.31
  450.1 3.7 copy-start.31
  457.3 3.7 copy-start.31
  471.6 207.3 %reduce-scatter.7.cloned.1.call-start = ((), (), s32[]{:S(2)}) async-start(), calls=%async_computation.14 | async-start | bytes 4718592 | tf_op jit(solution)/shard_map/reduce_scatter | solution.py:289
  479.6 256.3 %reduce-scatter.11.cloned.1.call-start = ((), (), s32[]{:S(2)}) async-start(), calls=%async_computation.16 | async-start | bytes 7208960 | tf_op jit(solution)/shard_map/reduce_scatter | solution.py:325
  485.3 399.7 %reduce-scatter.9.cloned.1.call-start = ((), (), s32[]{:S(2)}) async-start(), calls=%async_computation.15 | async-start | bytes 24903680 | tf_op jit(solution)/shard_map/reduce_scatter | solution.py:319
  495.2 93.1 %copy-start.28 = (f32[256,128]{0,1:T(8,128)S(1)}, f32[256,128]{0,1:T(8,128)}, u32[]{:S(2)}) copy-start(f32[256,128]{0,1:T(8,128)} %get-tuple-element.1104) | copy-start | bytes 393220
  495.2 93.1 %copy-start.29 = (f32[256,128]{0,1:T(8,128)S(1)}, f32[256,128]{0,1:T(8,128)}, u32[]{:S(2)}) copy-start(f32[256,128]{0,1:T(8,128)} %get-tuple-element.1102) | copy-start | bytes 393220
  686.0 4.1 copy-start.11
  688.5 3.3 copy-start.9
  690.2 3.3 copy-start.34
  690.2 3.3 copy-start.48
  693.5 4.2 copy-start.46
  702.2 182.9 %copy-start.7 = (bf16[1024,1024]{1,0:T(8,128)(2,1)S(1)}, bf16[1024,1024]{1,0:T(8,128)(2,1)}, u32[]{:S(2)}) copy-start(bf16[1024,1024]{1,0:T(8,128)(2,1)} %all-gather.14.cloned.1.call-done) | copy-start | bytes 6291460
  702.2 405.2 %all-reduce.3.cloned.1.call-start = ((), (), s32[]{:S(2)}) async-start(), calls=%async_computation.17 | async-start | bytes 12845056 | tf_op jit(solution)/shard_map/psum | solution.py:332
  885.1 3.5 copy-start.19
  885.1 3.5 copy-start.21
  886.7 47.0 %copy-start.6 = (f32[256,1024]{1,0:T(8,128)S(1)}, f32[256,1024]{1,0:T(8,128)}, u32[]{:S(2)}) copy-start(f32[256,1024]{1,0:T(8,128)} %copy-done.5) | copy-start | bytes 3145732
  1107.4 3.9 copy-start.4
  (33 other events, 68.4 us)
Sparse Core Ops, SparseCore 0:
  9.6 25.2 all-gather.13
  36.5 22.5 all-gather.9
  60.6 22.5 all-gather.15
  85.8 73.3 all-gather.11
  161.8 71.6 all-gather.17
  234.9 20.8 all-gather.19
  257.4 43.3 all-gather.21
  302.4 43.3 all-gather.23
  347.4 43.3 all-gather.25
  471.7 115.1 reduce-scatter.4
  591.0 87.8 reduce-scatter.6
  681.3 54.5 reduce-scatter.10
  738.7 146.2 reduce-scatter.8
  888.9 218.4 all-reduce.2
where the time goes:
time: 1130 us; the launch traced here: 1120 us
  waiting for transfers between devices  824 us (73%)
  local copies, waits for them, and re-layouts  97.8 us (9%)
  matrix products  83.8 us (7%)
  other arithmetic  46.4 us (4%)
  blocking collectives  43.4 us (4%)
  between operations  15 us (1%)
  loops' own time  11.6 us (1%)
    psum x1, waiting for transfers between devices, shards(): lax.psum(wide_local, 'ctx').astype(jnp.float32)  172 us
    reduce_scatter x1, waiting for transfers between devices, shards(): lax.psum_scatter(wide_term(lambda operand: operand).astype(jnp.bfloat16),...  149 us
    reduce_scatter x1, waiting for transfers between devices, shards(): lax.psum_scatter(key_terms.astype(jnp.bfloat16), 'ctx', scatter_dimension...  90.5 us
    reduce_scatter x1, waiting for transfers between devices, shards(): lax.psum_scatter(value_terms.astype(jnp.bfloat16), 'ctx', scatter_dimensi...  73.9 us
    all_gather x1, waiting for transfers between devices, shards(): lax.all_gather(values_local, 'ctx', axis=0, tiled=True)  68 us
    all_gather x1, waiting for transfers between devices, shards(): lax.all_gather(keys_local, 'ctx', axis=0, tiled=True)  66.9 us
    psum x1, blocking collectives, shards(): lax.psum(jnp.stack([grad_norm_one, grad_norm_two, grad_norm_three, grad_n...  43.4 us
    all_gather x1, waiting for transfers between devices, shards(): lax.all_gather(w_up, 'fsdp', axis=0, tiled=True)  39 us
  transfers between devices with their start and end apart: 14, of which 13 were waited for; matrix products, arithmetic and copies ran while one was open for 12% of the time, Pallas kernels for 0%

commit v1 on v0

--- a/solution.py
+++ b/solution.py
@@ -85,6 +85,11 @@
     group_ids,
     cont_ids,
 ):
+
+    def _form_chains(frame, across):
+        z1 = lax.all_gather(frame, axis_name=across).sum(axis=0)
+        return z1
+
     local_rows = block_in.shape[1]
     model_width = block_in.shape[2]
     ff_width = w_gate.shape[1]
@@ -329,7 +334,7 @@
         tiled=True,
     )
     wide_sum, ff_sum = (
-        lax.psum(wide_local, "ctx").astype(jnp.float32),
+        _form_chains(wide_local, "ctx").astype(jnp.float32),
         lax.psum(ff_local, "ctx").astype(jnp.float32),
     )
     gain_sums = lax.psum(

time: 1130 us -> 1770 us (1.57)
  waiting for transfers between devices: 824 us -> 1450 us
  other arithmetic: 46.4 us -> 64.3 us
    all_gather x0 -> x1, waiting for transfers between devices: none -> 753 us  [_form_chains(): z1 = lax.all_gather(frame, axis_name=across).sum(axis=0)]
    psum x1, waiting for transfers between devices: 172 us -> 42.9 us  [shards(): lax.psum(ff_local, 'ctx').astype(jnp.float32)]
  transfers between devices with their start and end apart: 14 -> 15, of which waited for: 13 -> 14; matrix products, arithmetic and copies ran while one was open for 12% -> 8% of each run, Pallas kernels for 0% -> 0%
where the time goes in v1:
time: 1770 us; the launch traced here: 1760 us
  waiting for transfers between devices  1450 us (82%)
  local copies, waits for them, and re-layouts  97.8 us (6%)
  matrix products  83.8 us (5%)
  other arithmetic  64.3 us (4%)
  blocking collectives  40.9 us (2%)
    all_gather x1, waiting for transfers between devices, _form_chains(): z1 = lax.all_gather(frame, axis_name=across).sum(axis=0)  753 us
    reduce_scatter x1, waiting for transfers between devices, shards(): lax.psum_scatter(wide_term(lambda operand: operand).astype(jnp.bfloat16),...  149 us
    reduce_scatter x1, waiting for transfers between devices, shards(): lax.psum_scatter(key_terms.astype(jnp.bfloat16), 'ctx', scatter_dimension...  90.5 us
    reduce_scatter x1, waiting for transfers between devices, shards(): lax.psum_scatter(value_terms.astype(jnp.bfloat16), 'ctx', scatter_dimensi...  73.7 us
    all_gather x1, waiting for transfers between devices, shards(): lax.all_gather(values_local, 'ctx', axis=0, tiled=True)  68 us
    all_gather x1, waiting for transfers between devices, shards(): lax.all_gather(keys_local, 'ctx', axis=0, tiled=True)  66.9 us
    psum x1, waiting for transfers between devices, shards(): lax.psum(ff_local, 'ctx').astype(jnp.float32)  42.9 us
    psum x1, blocking collectives, shards(): lax.psum(jnp.stack([grad_norm_one, grad_norm_two, grad_norm_three, grad_n...  40.9 us
  transfers between devices with their start and end apart: 15, of which 14 were waited for; matrix products, arithmetic and copies ran while one was open for 8% of the time, Pallas kernels for 0%

profile of v1, /device:TPU:0, one launch (start us, length us, event | category | flops | bytes accessed | tf_op | source)
XLA Modules:
  0.0 1762.0 jit_solution(17170568376648721349)
XLA Ops:
  16.3 18.6 %all-gather.16.cloned.1.call-done = bf16[1024,1024]{1,0:T(8,128)(2,1)} async-done(((bf16[256,1024]{1,0:T(8,128)(2,1)}), bf16[1024,1024]{1,0:T(8,128)(2,1)}) %all-gather.16.cloned.1.call-update) | async-done | bytes 2097168 | tf_op jit(solution)/shard_map/all_gather | solution.py:119
  37.8 21.3 %all-gather.12.cloned.1.call-done = bf16[1024,1024]{1,0:T(8,128)(2,1)} async-done(((bf16[256,1024]{1,0:T(8,128)(2,1)}), bf16[1024,1024]{1,0:T(8,128)(2,1)}) %all-gather.12.cloned.1.call-update) | async-done | bytes 2097168 | tf_op jit(solution)/shard_map/all_gather | solution.py:120
  59.1 3.9 copy.83
  67.9 15.3 all-gather.18.cloned.1.call-done
  83.3 3.1 convolution_convert_fusion.6
  92.4 66.9 %all-gather.14.cloned.1.call-done = bf16[2048,1024]{1,0:T(8,128)(2,1)} async-done(((bf16[256,1024]{1,0:T(8,128)(2,1)}), bf16[2048,1024]{1,0:T(8,128)(2,1)}) %all-gather.14.cloned.1.call-update) | async-done | bytes 4194320 | tf_op jit(solution)/shard_map/all_gather | solution.py:136
  159.2 3.3 copy.128
  162.5 3.0 copy.88
  165.5 68.0 %all-gather.20.cloned.1.call-done = bf16[2048,1024]{1,0:T(8,128)(2,1)} async-done(((bf16[256,1024]{1,0:T(8,128)(2,1)}), bf16[2048,1024]{1,0:T(8,128)(2,1)}) %all-gather.20.cloned.1.call-update) | async-done | bytes 4194320 | tf_op jit(solution)/shard_map/all_gather | solution.py:137
  233.5 3.3 copy.129
  239.6 10.0 while.63
  241.3 3.1 conditional.16
  249.7 10.7 while.64
  251.5 3.6 conditional.17
  251.5 3.6 fusion.24
  267.4 33.4 %all-gather.24.cloned.1.call-done = bf16[1024,2816]{1,0:T(8,128)(2,1)} async-done(((bf16[256,2816]{1,0:T(8,128)(2,1)}), bf16[1024,2816]{1,0:T(8,128)(2,1)}) %all-gather.24.cloned.1.call-update) | async-done | bytes 5767184 | tf_op jit(solution)/shard_map/all_gather | solution.py:208
  300.8 6.0 fusion.145
  306.8 39.0 %all-gather.26.cloned.1.call-done = bf16[1024,2816]{1,0:T(8,128)(2,1)} async-done(((bf16[256,2816]{1,0:T(8,128)(2,1)}), bf16[1024,2816]{1,0:T(8,128)(2,1)}) %all-gather.26.cloned.1.call-update) | async-done | bytes 5767184 | tf_op jit(solution)/shard_map/all_gather | solution.py:209
  345.8 7.4 multiply_convert_fusion.3
  353.2 37.6 %all-gather.28.cloned.1.call-done = bf16[2816,1024]{1,0:T(8,128)(2,1)} async-done(((bf16[704,1024]{1,0:T(8,128)(2,1)}), bf16[2816,1024]{1,0:T(8,128)(2,1)}) %all-gather.28.cloned.1.call-update) | async-done | bytes 5767184 | tf_op jit(solution)/shard_map/all_gather | solution.py:210
  390.8 5.0 multiply_reduce_fusion.4
  398.1 6.1 multiply_convert_fusion.1
  410.5 11.4 while.65
  412.2 4.5 conditional.18
  423.0 38.2 %while.66 = (s32[]{:T(128)}, f32[256,8,128]{2,0,1:T(8,128)}, f32[4,512,8,128]{3,1,2,0:T(8,128)}, bf16[4,512,8,128]{3,1,2,0:T(8,128)(2,1)}, pred[256]{0:T(512)(12...) while((s32[]{:T(128)}, f32[256,8,128]{2,0,1:T(8,128)}, ...), condition=%wide.region_36.37_spmd.clone.clone, body=%wide.region_32.36_spmd.clone.clone.sunk | while | flops 1353846528 | bytes 89568512 | solution.py:285
  424.7 9.5 conditional.19
  461.2 4.6 multiply_convert_fusion
  468.5 3.2 copy.136
  471.7 4.9 copy.108
  476.6 3.0 copy.135
  481.1 4.2 convolution_convert_fusion
  487.9 3.1 convolution_convert_fusion.2
  491.1 4.1 copy.112
  496.4 90.5 %reduce-scatter.5.cloned.1.call-done = bf16[256,1024]{1,0:T(8,128)(2,1)} async-done(((bf16[2048,1024]{1,0:T(8,128)(2,1)}), bf16[256,1024]{1,0:T(8,128)(2,1)}) %reduce-scatter.5.cloned.1.call-update) | async-done | bytes 524304 | tf_op jit(solution)/shard_map/reduce_scatter | solution.py:291
  601.1 3.9 copy.110
  605.0 73.7 %reduce-scatter.7.cloned.1.call-done = bf16[256,1024]{1,0:T(8,128)(2,1)} async-done(((bf16[2048,1024]{1,0:T(8,128)(2,1)}), bf16[256,1024]{1,0:T(8,128)(2,1)}) %reduce-scatter.7.cloned.1.call-update) | async-done | bytes 524304 | tf_op jit(solution)/shard_map/reduce_scatter | solution.py:294
  678.7 3.2 convolution_convert_fusion.3
  681.9 3.9 copy.111
  693.3 4.2 convert_dynamic-update-slice_fusion.1
  697.5 4.5 convert_dynamic-update-slice_fusion
  702.1 33.7 %reduce-scatter.11.cloned.1.call-done = bf16[704,1024]{1,0:T(8,128)(2,1)} async-done(((bf16[2816,1024]{1,0:T(8,128)(2,1)}), bf16[704,1024]{1,0:T(8,128)(2,1)}) %reduce-scatter.11.cloned.1.call-update) | async-done | bytes 1441808 | tf_op jit(solution)/shard_map/reduce_scatter | solution.py:330
  735.8 149.0 %reduce-scatter.9.cloned.1.call-done = bf16[256,9728]{1,0:T(8,128)(2,1)} async-done(((bf16[1024,9728]{1,0:T(8,128)(2,1)}), bf16[256,9728]{1,0:T(8,128)(2,1)}) %reduce-scatter.9.cloned.1.call-update) | async-done | bytes 4980752 | tf_op jit(solution)/shard_map/reduce_scatter | solution.py:324
  889.6 40.9 %psum.14 = f32[4,1024]{1,0:T(4,128)S(1)} all-reduce(f32[4,1024]{1,0:T(4,128)S(1)} %pad_maximum_fusion.2), channel_id=1, replica_groups=mesh['ctx'=8,'fsdp'=4] {'ctx','fsdp'}, use_global_device_ids=true, to_apply=%region_46.47 | all-reduce | flops 4096 | bytes 32768 | tf_op jit(solution)/shard_map/psum | solution.py:340
  932.4 42.9 %all-reduce.2.cloned.1.call-done = bf16[704,1024]{1,0:T(8,128)(2,1)} async-done(((bf16[704,1024]{1,0:T(8,128)(2,1)}), bf16[704,1024]{1,0:T(8,128)(2,1)}) %all-reduce.2.cloned.1.call-update) | async-done | bytes 1441808 | tf_op jit(solution)/shard_map/psum | solution.py:338
  975.3 3.3 convert_element_type.196
  978.6 753.2 %all-gather.30.cloned.1.call-done = bf16[2048,9728]{1,0:T(8,128)(2,1)} async-done(((bf16[256,9728]{1,0:T(8,128)(2,1)}), bf16[2048,9728]{1,0:T(8,128)(2,1)}) %all-gather.30.cloned.1.call-update) | async-done | bytes 39845904 | tf_op jit(solution)/shard_map/all_gather | solution.py:90
  1731.8 16.6 reduce_sum.222
  1748.4 3.9 fusion.143
  (352 shorter events, 137.2 us)
Async XLA Ops:
  7.2 27.7 %all-gather.16.cloned.1.call-start = ((), (), s32[]{:S(2)}) async-start(), calls=%async_computation.6 | async-start | bytes 2621440 | tf_op jit(solution)/shard_map/all_gather | solution.py:119
  7.9 51.2 %all-gather.12.cloned.1.call-start = ((), (), s32[]{:S(2)}) async-start(), calls=%async_computation.4 | async-start | bytes 2621440 | tf_op jit(solution)/shard_map/all_gather | solution.py:120
  8.7 74.6 %all-gather.18.cloned.1.call-start = ((), (), s32[]{:S(2)}) async-start(), calls=%async_computation.7 | async-start | bytes 2621440 | tf_op jit(solution)/shard_map/all_gather | solution.py:121
  9.4 149.9 %all-gather.14.cloned.1.call-start = ((), (), s32[]{:S(2)}) async-start(), calls=%async_computation.5 | async-start | bytes 4718592 | tf_op jit(solution)/shard_map/all_gather | solution.py:136
  15.0 51.4 %copy-start.25 = (f32[256,128]{0,1:T(8,128)}, f32[256,128]{0,1:T(8,128)S(1)}, u32[]{:S(2)}) copy-start(f32[256,128]{0,1:T(8,128)S(1)} %get-tuple-element.1101) | copy-start | bytes 393220
  16.3 67.0 %copy-start.36 = (f32[256]{0:T(256)}, f32[256]{0:T(256)S(1)}, u32[]{:S(2)}) copy-start(f32[256]{0:T(256)S(1)} %add_rsqrt_fusion.3) | copy-start | bytes 3076
  34.9 28.1 %copy-start.4 = (bf16[1,256,1024]{2,1,0:T(8,128)(2,1)S(1)}, bf16[1,256,1024]{2,1,0:T(8,128)(2,1)}, u32[]{:S(2)}) copy-start(bf16[1,256,1024]{2,1,0:T(8,128)(2,1)} %param.33) | copy-start | bytes 1572868
  34.9 28.1 %copy-start.34 = (f32[1024]{0:T(1024)S(1)}, f32[1024]{0:T(1024)}, u32[]{:S(2)}) copy-start(f32[1024]{0:T(1024)} %param.39) | copy-start | bytes 12292
  67.9 22.3 %copy-start.42 = (s32[4,2]{0,1:T(2,128)S(1)}, s32[4,2]{0,1:T(2,128)}, u32[]{:S(2)}) copy-start(s32[4,2]{0,1:T(2,128)} %param.47) | copy-start | bytes 100
  67.9 22.3 %copy-start.43 = (s32[4,2]{0,1:T(2,128)S(1)}, s32[4,2]{0,1:T(2,128)}, u32[]{:S(2)}) copy-start(s32[4,2]{0,1:T(2,128)} %param.49) | copy-start | bytes 100
  67.9 165.6 %all-gather.20.cloned.1.call-start = ((), (), s32[]{:S(2)}) async-start(), calls=%async_computation.8 | async-start | bytes 4718592 | tf_op jit(solution)/shard_map/all_gather | solution.py:137
  86.4 176.7 %all-gather.22.cloned.1.call-start = ((), (), s32[]{:S(2)}) async-start(), calls=%async_computation.9 | async-start | bytes 2621440 | tf_op jit(solution)/shard_map/all_gather | solution.py:122
  87.0 213.8 %all-gather.24.cloned.1.call-start = ((), (), s32[]{:S(2)}) async-start(), calls=%async_computation.10 | async-start | bytes 7208960 | tf_op jit(solution)/shard_map/all_gather | solution.py:208
  87.8 258.0 %all-gather.26.cloned.1.call-start = ((), (), s32[]{:S(2)}) async-start(), calls=%async_computation.11 | async-start | bytes 7208960 | tf_op jit(solution)/shard_map/all_gather | solution.py:209
  88.5 302.3 %all-gather.28.cloned.1.call-start = ((), (), s32[]{:S(2)}) async-start(), calls=%async_computation.12 | async-start | bytes 7208960 | tf_op jit(solution)/shard_map/all_gather | solution.py:210
  89.3 497.7 %reduce-scatter.5.cloned.1.call-start = ((), (), s32[]{:S(2)}) async-start(), calls=%async_computation.13 | async-start | bytes 4718592 | tf_op jit(solution)/shard_map/reduce_scatter | solution.py:291
  260.5 5.5 copy-start.38
  261.8 4.6 copy-start.39
  390.8 7.3 slice-start.4
  390.8 5.0 copy-start.12
  390.8 5.0 copy-start.41
  390.8 7.3 slice-start.5
  396.8 7.4 slice-start
  396.8 9.1 slice-start.2
  398.1 6.1 copy-start.23
  398.1 6.1 slice-start.1
  398.1 7.8 slice-start.3
  424.7 4.7 copy-start.31
  435.6 3.7 copy-start.30
  442.8 3.8 copy-start.30
  450.1 3.7 copy-start.30
  457.3 3.7 copy-start.30
  471.7 207.0 %reduce-scatter.7.cloned.1.call-start = ((), (), s32[]{:S(2)}) async-start(), calls=%async_computation.14 | async-start | bytes 4718592 | tf_op jit(solution)/shard_map/reduce_scatter | solution.py:294
  479.7 256.1 %reduce-scatter.11.cloned.1.call-start = ((), (), s32[]{:S(2)}) async-start(), calls=%async_computation.16 | async-start | bytes 7208960 | tf_op jit(solution)/shard_map/reduce_scatter | solution.py:330
  485.3 399.5 %reduce-scatter.9.cloned.1.call-start = ((), (), s32[]{:S(2)}) async-start(), calls=%async_computation.15 | async-start | bytes 24903680 | tf_op jit(solution)/shard_map/reduce_scatter | solution.py:324
  495.2 93.1 %copy-start.27 = (f32[256,128]{0,1:T(8,128)S(1)}, f32[256,128]{0,1:T(8,128)}, u32[]{:S(2)}) copy-start(f32[256,128]{0,1:T(8,128)} %get-tuple-element.1102) | copy-start | bytes 393220
  495.2 93.1 %copy-start.28 = (f32[256,128]{0,1:T(8,128)S(1)}, f32[256,128]{0,1:T(8,128)}, u32[]{:S(2)}) copy-start(f32[256,128]{0,1:T(8,128)} %get-tuple-element.1100) | copy-start | bytes 393220
  685.8 4.1 copy-start.11
  688.3 3.4 copy-start.9
  689.9 3.4 copy-start.47
  693.3 4.2 copy-start.45
  702.0 182.9 %copy-start.7 = (bf16[1024,1024]{1,0:T(8,128)(2,1)S(1)}, bf16[1024,1024]{1,0:T(8,128)(2,1)}, u32[]{:S(2)}) copy-start(bf16[1024,1024]{1,0:T(8,128)(2,1)} %all-gather.16.cloned.1.call-done) | copy-start | bytes 6291460
  702.0 273.2 %all-reduce.2.cloned.1.call-start = ((), (), s32[]{:S(2)}) async-start(), calls=%async_computation.17 | async-start | bytes 2883584 | tf_op jit(solution)/shard_map/psum | solution.py:338
  735.8 996.0 %all-gather.30.cloned.1.call-start = ((), (), s32[]{:S(2)}) async-start(), calls=%async_computation.18 | async-start | bytes 44826624 | tf_op jit(solution)/shard_map/all_gather | solution.py:90
  884.9 3.5 copy-start.19
  884.9 3.5 copy-start.21
  886.5 44.6 %copy-start.6 = (f32[256,1024]{1,0:T(8,128)S(1)}, f32[256,1024]{1,0:T(8,128)}, u32[]{:S(2)}) copy-start(f32[256,1024]{1,0:T(8,128)} %copy-done.5) | copy-start | bytes 3145732
  1748.4 3.9 copy-start.3
  (33 other events, 68.9 us)
Sparse Core Ops, SparseCore 0:
  9.6 25.2 all-gather.15
  36.5 22.5 all-gather.11
  60.6 22.5 all-gather.17
  85.8 73.3 all-gather.13
  161.8 71.6 all-gather.19
  234.9 20.8 all-gather.21
  257.4 43.3 all-gather.23
  302.4 43.3 all-gather.25
  347.4 43.3 all-gather.27
  471.8 115.1 reduce-scatter.4
  591.0 87.6 reduce-scatter.6
  681.1 54.6 reduce-scatter.10
  738.5 146.2 reduce-scatter.8
  888.4 86.8 all-reduce.1
  976.7 754.9 all-gather.29
